TPU v7x, 256 devices: a whole 4x4x8 slice. The times are simulated.
256 devices in a mesh: pair: 64 (over y, z, core), virt: 4 (over x).
Axes of the slice: x: 4, y: 4, z: 8, core: 2. Of those that a mesh axis runs over, the one named last changes fastest.
Arguments:
- amplitudes: bfloat16 [2048, 128, 1024], P('pair', 'virt'), may hold values from -6 to 6
- amp_pairs: int32 [2048], P('pair'), may hold values from 0 to 16383, as said below
- pair_map: int32 [16384], replicated, may hold values from -1 to 511, as said below
- integrals: bfloat16 [512, 2, 1024, 1024], P('pair', None, None, 'virt'), may hold values from -0.1875 to 0.1875
- block_cols: int32 [512, 2], P('pair'), may hold values from 0 to 16383, as said below
- occ_energy: float32 [8192], P('pair'), may hold values from -3 to -0.7
- virt_energy: float32 [4096], replicated, may hold values from 0.3 to 2
Outputs:
- update: bfloat16 [2048, 128, 1024], P('pair', None, 'virt')
Inputs may be any that keep to these rules, and one draw needn't show every extreme that they name: `amp_pairs`: within one occupied tile (tiles k * 32 to k * 32 + 31) the pairs differ and each has a row in pair_map. Consecutive occupied tiles form groups that hold the same set of pairs, and a pair belongs to one group only. `pair_map`: exactly 512 entries are not -1: the rows 0 to 511, once each, at the pairs that occur in amp_pairs. Row u lies on pair index u // 8. The pairs of one occupied tile have at most 1 row on any one pair index, and some reach 1. At most 8 occupied tiles hold the pair of any one row, and some row is held by exactly 8. `block_cols`: the 2 entries of a row differ, and each is a pair of the group of occupied tiles that holds the row's own pair.
All inputs are finite; a program needn't handle non-finite values.
Results may differ from a plain program's by a relative error of at most 0.0049.
Values may be sent and summed in bfloat16 or wider, within the bound.
A program may use at most 128 MiB of HBM per device.

v0:
```python
import jax
import jax.numpy as jnp
from jax import lax
from jax.sharding import PartitionSpec as P

VTILE = 32


def local(amplitudes, amp_pairs, pair_map, integrals, block_cols, occ_energy, virt_energy):
    tile_count = amplitudes.shape[0]
    pair_devices = lax.axis_size("pair")
    virt_devices = lax.axis_size("virt")
    capacity = -(-tile_count // pair_devices)
    row_limit = min(8, pair_devices - pair_devices // 4 + 1)
    local_rows = integrals.shape[0]
    block_count = integrals.shape[1]
    full_width = integrals.shape[2]
    part_width = integrals.shape[3]
    occ_rows = occ_energy.shape[0]
    send_slots = pair_devices * capacity
    row_of_tile = pair_map[amp_pairs]
    present = row_of_tile >= 0
    owner_pair = row_of_tile // local_rows
    order_index = jnp.arange(tile_count, dtype=jnp.int32)
    earlier = (
        (owner_pair[:, None] == owner_pair[None, :])
        & (order_index[None, :] < order_index[:, None])
        & present[None, :]
    )
    slot_rank = jnp.sum(earlier.astype(jnp.int32), axis=1)
    destination = jnp.where(present, owner_pair * capacity + slot_rank, send_slots)
    target_rows = (
        jnp.full((send_slots,), -1, jnp.int32)
        .at[destination]
        .set(row_of_tile % local_rows, mode="drop")
    )
    sender_pairs = jnp.broadcast_to(amp_pairs[None, None, :], (pair_devices, capacity, tile_count))
    local_row_ids = jnp.arange(local_rows, dtype=jnp.int32)
    outgoing = lax.all_gather(amplitudes, "virt", axis=1, tiled=True)
    send_tiles = (
        jnp.zeros((send_slots,) + outgoing.shape[1:], jnp.bfloat16)
        .at[destination]
        .set(outgoing, mode="drop")
    )
    packed = (
        send_tiles.reshape((pair_devices, capacity) + outgoing.shape[1:]),
        target_rows.reshape(pair_devices, capacity),
        sender_pairs,
    )
    arrived = lax.all_to_all(packed[0], "pair", split_axis=0, concat_axis=0, tiled=True)
    arrived_rows = lax.all_to_all(packed[1], "pair", split_axis=0, concat_axis=0, tiled=True)
    arrived_pairs = lax.all_to_all(packed[2], "pair", split_axis=0, concat_axis=0, tiled=True)
    sources = arrived.shape[0]
    item_count = arrived.shape[1]
    slot_total = sources * item_count
    tile_height = arrived.shape[2]
    flat_tiles = arrived.reshape(slot_total, tile_height, full_width)
    flat_rows = arrived_rows.reshape(slot_total)
    flat_pairs = arrived_pairs.reshape(slot_total, tile_count)
    slot_index = jnp.arange(slot_total, dtype=jnp.int32)
    limit_index = jnp.arange(row_limit, dtype=jnp.int32)

    def row_step(row_index, products):
        hit_mask = flat_rows == row_index
        hit_rank = jnp.cumsum(hit_mask.astype(jnp.int32)) - 1
        picked = hit_mask[None, :] & (hit_rank[None, :] == limit_index[:, None])
        occupied = jnp.any(picked, axis=1)
        chosen_slot = jnp.sum(picked.astype(jnp.int32) * slot_index[None, :], axis=1)
        gathered = flat_tiles[chosen_slot].reshape(row_limit * tile_height, full_width)
        row_blocks = lax.dynamic_index_in_dim(integrals, row_index, 0, keepdims=False)
        result = jnp.einsum("kd,mdc->kmc", gathered, row_blocks, preferred_element_type=jnp.float32)
        result = result.astype(jnp.bfloat16).reshape(
            row_limit, tile_height, block_count, part_width
        )
        return products.at[jnp.where(occupied, chosen_slot, slot_total)].set(result, mode="drop")

    empty_products = jnp.zeros((slot_total, tile_height, block_count, part_width), jnp.bfloat16)
    products = lax.fori_loop(0, local_rows, row_step, empty_products)
    row_hot = (flat_rows[:, None] == local_row_ids[None, :]).astype(jnp.int32)
    column_pair = jnp.sum(row_hot[:, :, None] * block_cols[None, :, :], axis=1)
    landing = flat_pairs[:, None, :] == column_pair[:, :, None]
    matched = jnp.any(landing, axis=2) & (flat_rows >= 0)[:, None]
    target = jnp.where(
        matched, jnp.sum(landing.astype(jnp.int32) * order_index[None, None, :], axis=2), tile_count
    )
    returned_back = (
        lax.all_to_all(
            products.reshape(sources, item_count, tile_height, block_count, part_width),
            "pair",
            split_axis=0,
            concat_axis=0,
            tiled=True,
        ),
        lax.all_to_all(
            target.reshape(sources, item_count, block_count),
            "pair",
            split_axis=0,
            concat_axis=0,
            tiled=True,
        ),
    )
    back_tiles, back_targets = returned_back
    landing_hot = (back_targets[None] == order_index[:, None, None, None]).astype(jnp.bfloat16)
    ladder = jnp.einsum(
        "apqm,pqimc->aic", landing_hot, back_tiles, preferred_element_type=jnp.float32
    )
    virt_tiles = virt_energy.shape[0] // VTILE
    energy_table = virt_energy.reshape(virt_tiles, VTILE)
    tile_ids = jnp.arange(virt_tiles, dtype=jnp.int32)
    onehot_first = (amp_pairs[:, None] // virt_tiles == tile_ids[None, :]).astype(jnp.float32)
    onehot_second = (amp_pairs[:, None] % virt_tiles == tile_ids[None, :]).astype(jnp.float32)
    energy_first = jnp.dot(onehot_first, energy_table, precision=lax.Precision.HIGHEST)
    energy_second = jnp.dot(onehot_second, energy_table, precision=lax.Precision.HIGHEST)
    per_device = VTILE // virt_devices
    energy_first = lax.dynamic_slice_in_dim(
        energy_first, lax.axis_index("virt") * per_device, per_device, 1
    )
    denominator = (
        energy_first[:, None, :, None]
        + energy_second[:, None, None, :]
        - occ_energy[None, :, None, None]
    )
    denominator = denominator.reshape(tile_count, occ_rows, part_width)
    return (ladder / denominator).astype(jnp.bfloat16)


def solution(mesh):
    in_specs = (
        P("pair", "virt", None),
        P("pair"),
        P(),
        P("pair", None, None, "virt"),
        P("pair", None),
        P("pair"),
        P(),
    )
    out_specs = P("pair", None, "virt")
    return jax.shard_map(local, mesh=mesh, in_specs=in_specs, out_specs=out_specs, check_vma=False)
```

profile of v0, /device:TPU:79, one launch (start us, length us, event | category | flops | bytes accessed | tf_op | source)
XLA Modules:
  0.0 841.0 jit_solution(6966731193070125893)
XLA Ops:
  6.5 0.7 all-gather.2.cloned.1.call-update
  7.3 0.7 and_select_fusion.1
  7.9 0.7 gather_fusion.1
  8.7 0.2 convert_reduce_fusion
  8.9 0.7 scatter_custom_fusion.1
  9.6 17.9 %all_to_all.29 = s32[64,1,1]{2,1,0:T(1,128)S(1)} all-to-all(s32[64,1,1]{2,1,0:T(1,128)S(1)} %copy.52), channel_id=1, replica_groups=mesh['pair'=64,'virt'=4] {'pair'}, dimensions={0} | all-to-all | bytes 512 | tf_op jit(solution)/shard_map/all_to_all | solution.py:51
  27.6 1.3 broadcast_in_dim.42
  28.9 7.5 all-to-all-start
  36.3 59.7 %all-gather.2.cloned.1.call-done = bf16[32,128,1024]{2,1,0:T(8,128)(2,1)} async-done(((bf16[32,32,1024]{2,1,0:T(8,128)(2,1)}), bf16[32,128,1024]{2,1,0:T(8,128)(2,1)}) %all-gather.2.cloned.1.call-update) | async-done | bytes 8388624 | tf_op jit(solution)/shard_map/all_gather | solution.py:39
  96.0 6.0 broadcast_in_dim.78
  102.0 21.4 %scatter_fusion.1 = bf16[64,128,1024]{2,1,0:T(8,128)(2,1)} fusion(bf16[64,128,1024]{2,1,0:T(8,128)(2,1)} %broadcast_in_dim.78, s32[32]{0:T(128)S(1)} %fusion.30, bf16[32,128,1024]{2,1,0:T(8,128)(2,1)} %all-gather.2.cloned.1.call-done), kind=kCustom, calls=%fused_computation.4 | custom fusion | bytes 25165952 | tf_op jit(solution)/shard_map/scatter | solution.py:43
  123.4 11.1 %all-to-all-start.3 = ((bf16[64,1,128,1024]{3,2,1,0:T(8,128)(2,1)}), bf16[64,1,128,1024]{3,2,1,0:T(8,128)(2,1)}, u32[]{:S(2)}, u32[]{:S(2)}) async-start(bf16[64,1,128,1024]{3,2,1,0:T(8,128)(2,1)} %bitcast.89), calls=%async_computation.3 | async-start | bytes 33554432 | tf_op jit(solution)/shard_map/all_to_all | solution.py:50
  134.5 1.2 reduce.1
  135.9 0.7 copy.53
  136.6 361.9 %all-to-all-done.3 = bf16[64,1,128,1024]{3,2,1,0:T(8,128)(2,1)} async-done(((bf16[64,1,128,1024]{3,2,1,0:T(8,128)(2,1)}), bf16[64,1,128,1024]{3,2,1,0:T(8,128)(2,1)}, u32[]{:S(2)}, u32[]{:S(2)}) %all-to-all-start.3) | async-done | bytes 16777248 | tf_op jit(solution)/shard_map/all_to_all | solution.py:50
  498.6 7.5 all-to-all-start.2
  506.1 4.3 broadcast_in_dim.47
  510.3 98.6 %while.16 = (s32[]{:T(128)}, bf16[64,128,2,256]{3,1,2,0:T(8,128)(2,1)}, s32[64]{0:T(128)S(1)}, bf16[64,128,1024]{2,1,0:T(8,128)(2,1)}, bf16[8,2,1024,256]{3,2,1,0:T(8,128)(2,1)}, /*index=5*/s32[]{:T(128)}, s32[]{:T(128)}) while((s32[]{:T(128)}, bf16[64,128,2,256]{3,1,2,0:T(8,128)(2,1)}, s32[64]{0:T(128)S(1)}, ...), condition=%wide.region_11.12_spmd.clone, body=%wide.region_6.11_spmd.clone.sunk | while | flops 1074274944 | bytes 13639173 | solution.py:78
  510.7 0.1 fusion.44
  510.8 0.1 fusion.43
  510.9 6.5 gather_fusion
  517.4 2.5 convolution_convert_fusion.2
  519.9 2.9 scatter_fusion
  523.1 0.1 fusion.44
  523.3 0.1 fusion.43
  523.4 6.5 gather_fusion
  529.9 2.5 convolution_convert_fusion.2
  532.4 2.7 scatter_fusion
  535.4 0.1 fusion.44
  535.5 0.1 fusion.43
  535.7 6.5 gather_fusion
  542.2 2.5 convolution_convert_fusion.2
  544.7 2.7 scatter_fusion
  547.7 0.1 fusion.44
  547.8 0.1 fusion.43
  548.0 6.5 gather_fusion
  554.4 2.5 convolution_convert_fusion.2
  557.0 2.7 scatter_fusion
  560.0 0.1 fusion.44
  560.2 0.1 fusion.43
  560.3 6.5 gather_fusion
  566.8 2.5 convolution_convert_fusion.2
  569.3 2.7 scatter_fusion
  572.3 0.1 fusion.44
  572.5 0.1 fusion.43
  572.6 6.5 gather_fusion
  579.1 2.5 convolution_convert_fusion.2
  581.6 2.7 scatter_fusion
  584.7 0.1 fusion.44
  584.9 6.5 gather_fusion
  591.4 2.5 convolution_convert_fusion.2
  594.0 2.7 scatter_fusion
  597.0 0.1 fusion.44
  597.2 6.5 gather_fusion
  603.7 2.5 convolution_convert_fusion.2
  606.3 2.7 scatter_fusion
  609.0 16.3 %copy.67 = bf16[64,128,2,256]{3,2,1,0:T(2,128)(2,1)} copy(bf16[64,128,2,256]{3,1,2,0:T(8,128)(2,1)} %get-tuple-element.181) | data formatting | bytes 16777216 | tf_op jit(solution)/shard_map/while | solution.py:78
  625.2 10.5 %all-to-all-start.4 = ((bf16[64,1,128,2,256]{4,3,2,1,0:T(2,128)(2,1)}), bf16[64,1,128,2,256]{4,3,2,1,0:T(2,128)(2,1)}, u32[]{:S(2)}, u32[]{:S(2)}) async-start(bf16[64,1,128,2,256]{4,3,2,1,0:T(2,128)(2,1)} %bitcast.91), calls=%async_computation.4 | async-start | bytes 16777216 | tf_op jit(solution)/shard_map/all_to_all | solution.py:87
  635.9 0.2 fusion.24
  636.2 0.2 fusion.25
  636.4 0.1 broadcast_add_fusion
  636.7 182.1 %all-to-all-done.4 = bf16[64,1,128,2,256]{4,3,2,1,0:T(2,128)(2,1)} async-done(((bf16[64,1,128,2,256]{4,3,2,1,0:T(2,128)(2,1)}), bf16[64,1,128,2,256]{4,3,2,1,0:T(2,128)(2,1)}, u32[]{:S(2)}, u32[]{:S(2)}) %all-to-all-start.4) | async-done | bytes 8388640 | tf_op jit(solution)/shard_map/all_to_all | solution.py:87
  818.8 12.9 %fusion.15 = bf16[32,128,256]{2,0,1:T(8,128)(2,1)S(1)} fusion(bf16[64,1,128,2,256]{4,3,2,1,0:T(2,128)(2,1)} %all-to-all-done.4, f32[128]{0:T(128)S(1)} %copy-done.4, f32[32,256]{1,0:T(8,128)S(1)} %add.165, s32[64,2]{0,1:T(2,128)S(1)} %bitcast.94), kind=kOutput, calls=%fused_computation.30 | convolution fusion | flops 271585280 | bytes 10519552 | tf_op jit(solution)/shard_map/apqm,pqimc->aic/dot_general | solution.py:104
  831.7 2.5 copy.58
  (88 shorter events, 4.0 us)
Async XLA Ops:
  6.5 1.4 copy-start
  6.5 89.5 %all-gather.2.cloned.1.call-start = ((), (), s32[]{:S(2)}) async-start(), calls=%async_computation.5 | async-start | bytes 10485760 | tf_op jit(solution)/shard_map/all_gather | solution.py:39
  28.9 94.5 %all-to-all-start = ((s32[64,1,32]{2,1,0:T(1,128)}), s32[64,1,32]{2,1,0:T(1,128)S(1)}, u32[]{:S(2)}, u32[]{:S(2)}) async-start(s32[64,1,32]{2,1,0:T(1,128)} %broadcast_in_dim.42), calls=%async_computation | async-start | bytes 65536 | tf_op jit(solution)/shard_map/all_to_all | solution.py:52
  123.4 12.3 %copy-start.3 = (s32[8,2]{0,1:T(2,128)S(1)}, s32[8,2]{0,1:T(2,128)}, u32[]{:S(2)}) copy-start(s32[8,2]{0,1:T(2,128)} %param.13) | copy-start | bytes 196
  123.4 375.2 %all-to-all-start.3 = ((bf16[64,1,128,1024]{3,2,1,0:T(8,128)(2,1)}), bf16[64,1,128,1024]{3,2,1,0:T(8,128)(2,1)}, u32[]{:S(2)}, u32[]{:S(2)}) async-start(bf16[64,1,128,1024]{3,2,1,0:T(8,128)(2,1)} %bitcast.89), calls=%async_computation.3 | async-start | bytes 33554432 | tf_op jit(solution)/shard_map/all_to_all | solution.py:50
  498.6 126.7 %all-to-all-start.2 = ((s32[64,1,2]{2,1,0:T(1,128)}), s32[64,1,2]{2,1,0:T(1,128)S(1)}, u32[]{:S(2)}, u32[]{:S(2)}) async-start(s32[64,1,2]{2,1,0:T(1,128)} %copy.53), calls=%async_computation.2 | async-start | bytes 65536 | tf_op jit(solution)/shard_map/all_to_all | solution.py:94
  625.2 10.6 %copy-start.2 = (f32[4096]{0:T(1024)S(1)}, f32[4096]{0:T(1024)}, u32[]{:S(2)}) copy-start(f32[4096]{0:T(1024)} %param.15) | copy-start | bytes 49156
  625.2 193.6 %copy-start.4 = (f32[128]{0:T(128)S(1)}, f32[128]{0:T(128)}, u32[]{:S(2)}) copy-start(f32[128]{0:T(128)} %param.14) | copy-start | bytes 1540
  625.2 193.6 %all-to-all-start.4 = ((bf16[64,1,128,2,256]{4,3,2,1,0:T(2,128)(2,1)}), bf16[64,1,128,2,256]{4,3,2,1,0:T(2,128)(2,1)}, u32[]{:S(2)}, u32[]{:S(2)}) async-start(bf16[64,1,128,2,256]{4,3,2,1,0:T(2,128)(2,1)} %bitcast.91), calls=%async_computation.4 | async-start | bytes 16777216 | tf_op jit(solution)/shard_map/all_to_all | solution.py:87
  818.8 15.4 %copy-start.1 = (s32[16384]{0:T(1024)S(1)}, s32[16384]{0:T(1024)}, u32[]{:S(2)}) copy-start(s32[16384]{0:T(1024)} %param.11) | copy-start | bytes 196612
Sparse Core Ops, SparseCore 0:
  9.2 86.8 all-gather.1
where the time goes:
time: 848 us; the launch traced here: 841 us
  waiting for transfers between devices  604 us (71%)
  local copies, waits for them, and re-layouts  129 us (15%)
  starting transfers between devices  36.6 us (4%)
  matrix products  33.1 us (4%)
  blocking collectives  17.9 us (2%)
  between operations  13.5 us (2%)
    all_to_all x1, waiting for transfers between devices, local(): lax.all_to_all(packed[0], 'pair', split_axis=0, concat_axis=0, tiled=True)  362 us
    all_to_all x1, waiting for transfers between devices, local(): lax.all_to_all(products.reshape(sources, item_count, tile_height, block_c...  182 us
    all_gather x1, waiting for transfers between devices, local(): outgoing = lax.all_gather(amplitudes, 'virt', axis=1, tiled=True)  59.7 us
    gather x8, local copies, waits for them, and re-layouts, row_step(): flat_tiles[chosen_slot].reshape(row_limit * tile_height, full_width)  51.6 us
    scatter x8, local copies, waits for them, and re-layouts, row_step(): products.at[jnp.where(occupied, chosen_slot, slot_total)]  21.8 us
    scatter x1, local copies, waits for them, and re-layouts, local(): send_tiles = jnp.zeros((send_slots,) + outgoing.shape[1:], jnp.bfloat16)....  21.4 us
    dot_general x8, matrix products, row_step(): jnp.einsum('kd,mdc->kmc', gathered, row_blocks, preferred_element_type=jn...  19.8 us
    all_to_all x1, blocking collectives, local(): lax.all_to_all(packed[1], 'pair', split_axis=0, concat_axis=0, tiled=True)  17.9 us
  transfers between devices with their start and end apart: 5, of which 3 were waited for; matrix products, arithmetic and copies ran while one was open for 18% of the time, Pallas kernels for 0%

commit v1 on v0

v1 whole, which is shorter than its diff:
```python
import functools

import jax
import jax.numpy as jnp
from jax import lax
from jax.experimental import pallas as pl
from jax.experimental.pallas import tpu as pltpu
from jax.sharding import PartitionSpec as P

VTILE = 32
MESH = pl.DeviceIdType.MESH
LANES = 128
LAG_RELAY, LAG_DOT, LAG_SEND = 3, 6, 7


def plan_kernel(local_rows, pair_map, amp_pairs, block_cols, tile_of_slot, meta):
    slots = tile_of_slot.shape[0]

    def clear(d, carry):
        tile_of_slot[d] = 0
        meta[0, 0, d] = -1
        return carry

    lax.fori_loop(0, slots, clear, 0)

    def place(j, carry):
        row = pair_map[amp_pairs[j]]

        @pl.when(row >= 0)
        def _():
            owner = lax.div(row, local_rows)
            tile_of_slot[owner] = j
            meta[0, 0, owner] = lax.rem(row, local_rows)

        return carry

    lax.fori_loop(0, amp_pairs.shape[0], place, 0)

    def copy(i, carry):
        meta[0, 0, slots + i] = block_cols[i]
        return carry

    lax.fori_loop(0, block_cols.shape[0], copy, 0)


def exchange_kernel(
    dims,
    tile_of_slot,
    meta_in,
    amplitudes,
    integrals,
    returned,
    meta_all,
    slots,
    gathered,
    blocks,
    products,
    meta_table,
    amp_send,
    amp_recv,
    right_send,
    left_send,
    relay_right_send,
    relay_left_send,
    from_left,
    from_right,
    relay_from_left,
    relay_from_right,
    product_send,
    product_recv,
    meta_send,
    meta_recv,
    load_sem,
):
    ny, nz, nc = dims
    n = ny * nz * nc
    me = lax.axis_index("pair")
    col = lax.axis_index("virt")
    nv = gathered.shape[1]
    height = gathered.shape[2]
    half = height // 2
    right, left, across = lax.rem(col + 1, nv), lax.rem(col + nv - 1, nv), lax.rem(col + 2, nv)
    my_y, my_z, my_c = lax.div(me, nz * nc), lax.rem(lax.div(me, nc), nz), lax.rem(me, nc)

    def partner(k, sign):
        i = lax.rem(k, nz)
        t = lax.div(i + 1, 2)
        odd = lax.rem(i, 2)
        dz = odd * t + (1 - odd) * lax.rem(nz - t, nz)
        dy = lax.rem(lax.div(k, nz), ny)
        dc = lax.div(k, nz * ny)
        y = lax.rem(my_y + sign * dy + ny, ny)
        z = lax.rem(my_z + sign * dz + nz, nz)
        c = lax.rem(my_c + dc, nc)
        return (y * nz + z) * nc + c

    def wait(ref, sem):
        pltpu.make_async_copy(ref, ref, sem).wait()

    load = pltpu.make_async_copy(integrals, blocks, load_sem)
    load.start()

    def fill(d, carry):
        slots[d] = amplitudes[tile_of_slot[d]]
        return carry

    lax.fori_loop(0, n, fill, 0)

    barrier = pltpu.get_barrier_semaphore()

    def greet(k, carry):
        pl.semaphore_signal(barrier, inc=1, device_id=(partner(k, 1), col), device_id_type=MESH)
        return carry

    lax.fori_loop(1, n, greet, 0)
    pl.semaphore_signal(barrier, inc=1, device_id=(me, right), device_id_type=MESH)
    pl.semaphore_signal(barrier, inc=1, device_id=(me, left), device_id_type=MESH)
    pl.semaphore_wait(barrier, n + 1)

    def send_meta(k, carry):
        pltpu.make_async_remote_copy(
            src_ref=meta_in.at[0],
            dst_ref=meta_all.at[me],
            send_sem=meta_send,
            recv_sem=meta_recv,
            device_id=(partner(k, 1), col),
            device_id_type=MESH,
        ).start()
        return carry

    lax.fori_loop(1, n, send_meta, 0)
    pltpu.make_async_copy(meta_in.at[0], meta_all.at[me], meta_recv).start()
    pltpu.make_async_copy(slots.at[me], gathered.at[me, col], amp_recv.at[0]).start()

    def send_slot(k, carry):
        target = partner(k, 1)
        pltpu.make_async_remote_copy(
            src_ref=slots.at[target],
            dst_ref=gathered.at[me, col],
            send_sem=amp_send,
            recv_sem=amp_recv.at[k],
            device_id=(target, col),
            device_id_type=MESH,
        ).start()
        return carry

    lax.fori_loop(1, n, send_slot, 0)

    wait(meta_all, meta_recv)
    table = pltpu.make_async_copy(meta_all, meta_table, load_sem)
    load.wait()
    table.start()
    table.wait()

    def along(ref, send_sem, recv_sem, target):
        pltpu.make_async_remote_copy(
            src_ref=ref,
            dst_ref=ref,
            send_sem=send_sem,
            recv_sem=recv_sem,
            device_id=(me, target),
            device_id_type=MESH,
        ).start()

    def step(t, carry):
        @pl.when(t < n)
        def _():
            own = gathered.at[partner(t, -1), col]
            wait(own, amp_recv.at[t])
            along(own, right_send, from_left.at[t], right)
            along(own, left_send, from_right.at[t], left)

        @pl.when((t >= LAG_RELAY) & (t < n + LAG_RELAY))
        def _():
            u = t - LAG_RELAY
            source = partner(u, -1)
            wait(gathered.at[source, left], from_left.at[u])
            along(
                gathered.at[source, left, pl.ds(0, half)], relay_right_send, relay_from_left.at[u], right
            )
            wait(gathered.at[source, right], from_right.at[u])
            along(
                gathered.at[source, right, pl.ds(half, half)], relay_left_send, relay_from_right.at[u], left
            )

        @pl.when((t >= LAG_DOT) & (t < n + LAG_DOT))
        def _():
            u = t - LAG_DOT
            source = partner(u, -1)
            wait(gathered.at[source, across, pl.ds(0, half)], relay_from_left.at[u])
            wait(gathered.at[source, across, pl.ds(half, half)], relay_from_right.at[u])
            row = jnp.maximum(meta_table[source, 0, me], 0)
            tile = gathered[source].reshape(nv * height, gathered.shape[3])
            for m in range(blocks.shape[1]):
                products[u, m] = jnp.dot(
                    tile, blocks[row, m], preferred_element_type=jnp.float32
                ).astype(jnp.bfloat16)

        @pl.when(t == LAG_SEND)
        def _():
            pltpu.make_async_copy(products.at[0], returned.at[me], product_recv).start()

        @pl.when(t > LAG_SEND)
        def _():
            u = t - LAG_SEND
            pltpu.make_async_remote_copy(
                src_ref=products.at[u],
                dst_ref=returned.at[me],
                send_sem=product_send,
                recv_sem=product_recv,
                device_id=(partner(u, -1), col),
                device_id_type=MESH,
            ).start()

        return carry

    lax.fori_loop(0, n + LAG_SEND, step, 0)

    wait(meta_all.at[pl.ds(0, n - 1)], meta_send)
    wait(slots.at[pl.ds(0, n - 1)], amp_send)
    wait(slots, right_send)
    wait(slots, left_send)
    wait(slots.at[pl.ds(0, n // 2)], relay_right_send)
    wait(slots.at[pl.ds(0, n // 2)], relay_left_send)
    wait(products.at[pl.ds(0, n - 1)], product_send)
    wait(returned, product_recv)


def combine_kernel(
    virt_tiles, amp_pairs, my_meta, meta_all, returned, first_table, second_table, occ, update, position, ladder
):
    step = pl.program_id(0)
    chunk = returned.shape[0]
    slots = meta_all.shape[0]

    @pl.when(step == 0)
    def _():
        def mark(j, carry):
            position[amp_pairs[j]] = j
            return carry

        lax.fori_loop(0, amp_pairs.shape[0], mark, 0)
        ladder[...] = jnp.zeros_like(ladder)

    def add(i, carry):
        slot = step * chunk + i
        row = my_meta[0, 0, slot]

        @pl.when(row >= 0)
        def _():
            for m in range(returned.shape[1]):
                target = position[meta_all[slot, 0, slots + row * returned.shape[1] + m]]
                ladder[target] += returned[i, m].astype(jnp.float32)

        return carry

    lax.fori_loop(0, chunk, add, 0)

    @pl.when(step == pl.num_programs(0) - 1)
    def _():
        def divide(j, carry):
            pair = amp_pairs[j]
            energy = (
                first_table[pl.ds(lax.div(pair, virt_tiles), 1), :]
                + second_table[pl.ds(lax.rem(pair, virt_tiles), 1), :]
            )
            update[j] = (ladder[j] / (energy - occ[...])).astype(update.dtype)
            return carry

        lax.fori_loop(0, amp_pairs.shape[0], divide, 0)


def pair_dims(n):
    return {64: (4, 8, 2), 8: (2, 2, 2), 4: (1, 2, 2)}[n]


def local(amplitudes, amp_pairs, pair_map, integrals, block_cols, occ_energy, virt_energy):
    tile_count, height, full_width = amplitudes.shape
    n = lax.axis_size("pair")
    nv = lax.axis_size("virt")
    local_rows, block_count, _, part_width = integrals.shape
    occ_rows = occ_energy.shape[0]
    smem = pl.BlockSpec(memory_space=pltpu.SMEM)
    vmem = pl.BlockSpec(memory_space=pltpu.VMEM)
    hbm = pl.BlockSpec(memory_space=pl.ANY)

    tile_of_slot, my_meta = pl.pallas_call(
        functools.partial(plan_kernel, local_rows),
        out_shape=(
            jax.ShapeDtypeStruct((n,), jnp.int32),
            jax.ShapeDtypeStruct((1, 1, LANES), jnp.int32),
        ),
        in_specs=[smem] * 3,
        out_specs=(smem, smem),
        name="plan",
    )(pair_map, amp_pairs, block_cols.reshape(-1))

    dma = pltpu.SemaphoreType.DMA
    returned, meta_all = pl.pallas_call(
        functools.partial(exchange_kernel, pair_dims(n)),
        out_shape=(
            jax.ShapeDtypeStruct((n, block_count, occ_rows, part_width), jnp.bfloat16),
            jax.ShapeDtypeStruct((n, 1, LANES), jnp.int32),
        ),
        in_specs=[smem, vmem, vmem, hbm],
        out_specs=(hbm, hbm),
        scratch_shapes=[
            pltpu.VMEM((n, height, full_width), jnp.bfloat16),
            pltpu.VMEM((n, nv, height, full_width), jnp.bfloat16),
            pltpu.VMEM(integrals.shape, jnp.bfloat16),
            pltpu.VMEM((n, block_count, occ_rows, part_width), jnp.bfloat16),
            pltpu.SMEM((n, 1, LANES), jnp.int32),
            dma,
            dma((n,)),
            dma,
            dma,
            dma,
            dma,
            dma((n,)),
            dma((n,)),
            dma((n,)),
            dma((n,)),
            dma,
            dma,
            dma,
            dma,
            dma,
        ],
        compiler_params=pltpu.CompilerParams(
            collective_id=0, has_side_effects=True, vmem_limit_bytes=60 * 2**20
        ),
        name="exchange",
    )(tile_of_slot, my_meta, amplitudes, integrals)

    virt_tiles = virt_energy.shape[0] // VTILE
    energy_table = virt_energy.reshape(virt_tiles, VTILE)
    per_device = VTILE // nv
    first = lax.dynamic_slice_in_dim(
        energy_table, lax.axis_index("virt") * per_device, per_device, 1
    )
    first_table = jnp.repeat(first, VTILE, axis=1)
    second_table = jnp.tile(energy_table, (1, per_device))
    chunk = min(8, n)
    whole = lambda *shape: pl.BlockSpec(shape, lambda i: (0,) * len(shape))
    return pl.pallas_call(
        functools.partial(combine_kernel, virt_tiles),
        out_shape=jax.ShapeDtypeStruct((tile_count, occ_rows, part_width), jnp.bfloat16),
        grid=(n // chunk,),
        in_specs=[
            smem,
            smem,
            smem,
            pl.BlockSpec((chunk, block_count, occ_rows, part_width), lambda i: (i, 0, 0, 0)),
            whole(virt_tiles, part_width),
            whole(virt_tiles, part_width),
            whole(occ_rows, 1),
        ],
        out_specs=whole(tile_count, occ_rows, part_width),
        scratch_shapes=[
            pltpu.SMEM((pair_map.shape[0],), jnp.int32),
            pltpu.VMEM((tile_count, occ_rows, part_width), jnp.float32),
        ],
        compiler_params=pltpu.CompilerParams(vmem_limit_bytes=32 * 2**20),
        name="combine",
    )(amp_pairs, my_meta, meta_all, returned, first_table, second_table, occ_energy[:, None])


def solution(mesh):
    in_specs = (
        P("pair", "virt", None),
        P("pair"),
        P(),
        P("pair", None, None, "virt"),
        P("pair", None),
        P("pair"),
        P(),
    )
    out_specs = P("pair", None, "virt")
    return jax.shard_map(local, mesh=mesh, in_specs=in_specs, out_specs=out_specs, check_vma=False)
```

time: 848 us -> 340 us (0.40)
  waiting for transfers between devices: 604 us -> 0 us
  Pallas kernels: 0 us -> 332 us
  local copies, waits for them, and re-layouts: 129 us -> 7.5 us
  starting transfers between devices: 36.6 us -> 0 us
  matrix products: 33.1 us -> 0 us
  blocking collectives: 17.9 us -> 0 us
  between operations: 13.5 us -> 0.08 us
    all_to_all x4 -> x0, waiting for transfers between devices: 544 us -> none  [the longest x1 362 us: local(): lax.all_to_all(packed[0], 'pair', split_axis=0, concat_axis=0, tiled=True)]
    pallas_call x0 -> x3, Pallas kernels: none -> 332 us  [the longest x1 321 us: local(): pl.pallas_call(functools.partial(exchange_kernel, pair_dims(n)), out_shap...]
    all_gather x1 -> x0, waiting for transfers between devices: 59.7 us -> none  [local(): outgoing = lax.all_gather(amplitudes, 'virt', axis=1, tiled=True)]
    gather x9 -> x0, local copies, waits for them, and re-layouts: 52.3 us -> none  [the longest x8 51.6 us: row_step(): flat_tiles[chosen_slot].reshape(row_limit * tile_height, full_width)]
    scatter x10 -> x0, local copies, waits for them, and re-layouts: 43.9 us -> none  [the longest x8 21.8 us: row_step(): products.at[jnp.where(occupied, chosen_slot, slot_total)]]
    all_to_all x4 -> x0, starting transfers between devices: 36.6 us -> none  [the longest x1 11.1 us: local(): lax.all_to_all(packed[0], 'pair', split_axis=0, concat_axis=0, tiled=True)]
    dot_general x11 -> x0, matrix products: 33.1 us -> none  [the longest x8 19.8 us: row_step(): jnp.einsum('kd,mdc->kmc', gathered, row_blocks, preferred_element_type=jn...]
    all_to_all x1 -> x0, blocking collectives: 17.9 us -> none  [local(): lax.all_to_all(packed[1], 'pair', split_axis=0, concat_axis=0, tiled=True)]
  transfers between devices with their start and end apart: 5 -> 0, of which waited for: 3 -> 0; matrix products, arithmetic and copies ran while one was open for 18% -> 0% of each run, Pallas kernels for 0% -> 0%
where the time goes in v1:
time: 340 us; the launch traced here: 339 us
  Pallas kernels  332 us (98%)
  local copies, waits for them, and re-layouts  7.5 us (2%)
    pallas_call x1, Pallas kernels, local(): pl.pallas_call(functools.partial(exchange_kernel, pair_dims(n)), out_shap...  321 us
    pallas_call x1, Pallas kernels, local(): pl.pallas_call(functools.partial(combine_kernel, virt_tiles), out_shape=j...  8.03 us

profile of v1, /device:TPU:79, one launch (start us, length us, event | category | flops | bytes accessed | tf_op | source)
XLA Modules:
  0.0 339.5 jit_solution(17437430045234259878)
XLA Ops:
  0.0 0.0 copy-start.2
  0.0 0.8 copy.10
  0.8 0.6 reshape.13.block_cols
  1.4 3.3 plan.1
  4.7 0.0 copy-start.3
  4.7 0.8 reshape.14
  5.5 0.1 copy.12
  5.5 0.1 constant_dynamic-slice_fusion
  5.6 0.1 copy.11
  5.7 0.8 copy.15.occ
  6.5 0.1 copy.14.second_table
  6.6 0.1 copy.13.first_table
  6.7 320.5 %exchange.1 = (bf16[64,2,128,256]{3,2,1,0:T(8,128)(2,1)}, s32[64,1,128]{2,1,0:T(1,128)}) custom-call(s32[64]{0:T(128)} %get-tuple-element.10.tile_of_slot, s32[1,1,128]{2,1,0:T(1,128)} %get-tuple-element.9.meta_in.my_meta, bf16[32,32,1024]{2,1,0:T(8,128)(2,1)} %amplitudes.1, bf16[8,2,1024,256]{3,2,1,0:T(8,128)(2,1)} %integrals.1), custom_call_target="tpu_custom_call" | custom-call | tf_op jit(solution)/shard_map/exchange/pallas_call | solution.py:299
  327.3 0.0 copy-done.2
  327.3 0.0 copy-done.3
  327.3 0.0 copy-start
  327.3 3.4 copy-done
  330.7 0.0 copy-start.1
  330.7 0.8 copy-done.1
  331.4 8.0 %combine.1 = bf16[32,128,256]{2,1,0:T(8,128)(2,1)} custom-call(s32[32]{0:T(128)S(1)} %copy-done.2, s32[1,1,128]{2,1,0:T(1,128)S(1)} %copy-done.3, s32[64,1,128]{2,1,0:T(1,128)S(1)} %copy-done.1, bf16[64,2,128,256]{3,2,1,0:T(8,128)(2,1)S(1)} %copy-done, f32[128,256]{1,0:T(8,128)S(1)} %copy.13.first_table, f32[128,256]{1,0:T(8,128)S(1)} %copy.14.second_table, ...), custom_call_target="tpu_custom_call" | custom-call | tf_op jit(solution)/shard_map/combine/pallas_call | solution.py:345
  (2 shorter events, 0.0 us)
Async XLA Ops:
  0.0 327.3 %copy-start.2 = (s32[32]{0:T(128)S(1)}, s32[32]{0:T(128)}, u32[]{:S(2)}) copy-start(s32[32]{0:T(128)} %amp_pairs.3) | copy-start | bytes 388
  4.7 322.6 %copy-start.3 = (s32[1,1,128]{2,1,0:T(1,128)S(1)}, s32[1,1,128]{2,1,0:T(1,128)}, u32[]{:S(2)}) copy-start(s32[1,1,128]{2,1,0:T(1,128)} %get-tuple-element.9.meta_in.my_meta) | copy-start | bytes 1540
  327.3 3.4 copy-start
  330.7 0.8 copy-start.1

commit v2 on v1

--- a/solution.py
+++ b/solution.py
@@ -51,6 +51,7 @@
     integrals,
     returned,
     meta_all,
+    targets,
     slots,
     gathered,
     blocks,
@@ -100,12 +101,6 @@
     load = pltpu.make_async_copy(integrals, blocks, load_sem)
     load.start()
 
-    def fill(d, carry):
-        slots[d] = amplitudes[tile_of_slot[d]]
-        return carry
-
-    lax.fori_loop(0, n, fill, 0)
-
     barrier = pltpu.get_barrier_semaphore()
 
     def greet(k, carry):
@@ -115,6 +110,13 @@
     lax.fori_loop(1, n, greet, 0)
     pl.semaphore_signal(barrier, inc=1, device_id=(me, right), device_id_type=MESH)
     pl.semaphore_signal(barrier, inc=1, device_id=(me, left), device_id_type=MESH)
+
+    def fill(d, carry):
+        slots[d] = amplitudes[tile_of_slot[d]]
+        return carry
+
+    lax.fori_loop(0, n, fill, 0)
+
     pl.semaphore_wait(barrier, n + 1)
 
     def send_meta(k, carry):
@@ -216,6 +218,17 @@
 
     lax.fori_loop(0, n + LAG_SEND, step, 0)
 
+    block_count = blocks.shape[1]
+
+    def find_targets(d, carry):
+        row = meta_table[me, 0, d]
+        for m in range(block_count):
+            pair = meta_table[d, 0, n + jnp.maximum(row, 0) * block_count + m]
+            targets[d * block_count + m] = jnp.where(row >= 0, pair, -1)
+        return carry
+
+    lax.fori_loop(0, n, find_targets, 0)
+
     wait(meta_all.at[pl.ds(0, n - 1)], meta_send)
     wait(slots.at[pl.ds(0, n - 1)], amp_send)
     wait(slots, right_send)
@@ -227,11 +240,10 @@
 
 
 def combine_kernel(
-    virt_tiles, amp_pairs, my_meta, meta_all, returned, first_table, second_table, occ, update, position, ladder
+    virt_tiles, amp_pairs, targets, returned, first_table, second_table, occ, update, position, ladder
 ):
     step = pl.program_id(0)
     chunk = returned.shape[0]
-    slots = meta_all.shape[0]
 
     @pl.when(step == 0)
     def _():
@@ -243,14 +255,12 @@
         ladder[...] = jnp.zeros_like(ladder)
 
     def add(i, carry):
-        slot = step * chunk + i
-        row = my_meta[0, 0, slot]
-
-        @pl.when(row >= 0)
+        first = (step * chunk + i) * returned.shape[1]
+
+        @pl.when(targets[first] >= 0)
         def _():
             for m in range(returned.shape[1]):
-                target = position[meta_all[slot, 0, slots + row * returned.shape[1] + m]]
-                ladder[target] += returned[i, m].astype(jnp.float32)
+                ladder[position[targets[first + m]]] += returned[i, m].astype(jnp.float32)
 
         return carry
 
@@ -296,14 +306,15 @@
     )(pair_map, amp_pairs, block_cols.reshape(-1))
 
     dma = pltpu.SemaphoreType.DMA
-    returned, meta_all = pl.pallas_call(
+    returned, _, targets = pl.pallas_call(
         functools.partial(exchange_kernel, pair_dims(n)),
         out_shape=(
             jax.ShapeDtypeStruct((n, block_count, occ_rows, part_width), jnp.bfloat16),
             jax.ShapeDtypeStruct((n, 1, LANES), jnp.int32),
+            jax.ShapeDtypeStruct((n * block_count,), jnp.int32),
         ),
         in_specs=[smem, vmem, vmem, hbm],
-        out_specs=(hbm, hbm),
+        out_specs=(hbm, hbm, smem),
         scratch_shapes=[
             pltpu.VMEM((n, height, full_width), jnp.bfloat16),
             pltpu.VMEM((n, nv, height, full_width), jnp.bfloat16),
@@ -349,7 +360,6 @@
         in_specs=[
             smem,
             smem,
-            smem,
             pl.BlockSpec((chunk, block_count, occ_rows, part_width), lambda i: (i, 0, 0, 0)),
             whole(virt_tiles, part_width),
             whole(virt_tiles, part_width),
@@ -362,7 +372,7 @@
         ],
         compiler_params=pltpu.CompilerParams(vmem_limit_bytes=32 * 2**20),
         name="combine",
-    )(amp_pairs, my_meta, meta_all, returned, first_table, second_table, occ_energy[:, None])
+    )(amp_pairs, targets, returned, first_table, second_table, occ_energy[:, None])
 
 
 def solution(mesh):

time: 340 us -> 337 us (level); the launches traced: 339 us -> 331 us
  Pallas kernels: 332 us -> 324 us
    pallas_call x1, Pallas kernels: 321 us -> 313 us  [local(): pl.pallas_call(functools.partial(exchange_kernel, pair_dims(n)), out_shap...]
where the time goes in v2:
time: 337 us; the launch traced here: 331 us
  Pallas kernels  324 us (96%)
  local copies, waits for them, and re-layouts  7.38 us (2%)
    pallas_call x1, Pallas kernels, local(): pl.pallas_call(functools.partial(exchange_kernel, pair_dims(n)), out_shap...  313 us
    pallas_call x1, Pallas kernels, local(): pl.pallas_call(functools.partial(combine_kernel, virt_tiles), out_shape=j...  7.42 us

profile of v2, /device:TPU:79, one launch (start us, length us, event | category | flops | bytes accessed | tf_op | source)
XLA Modules:
  0.0 331.2 jit_solution(13188651916234388296)
XLA Ops:
  0.0 0.0 copy-start.1
  0.0 0.8 copy.10
  0.8 0.6 reshape.13.block_cols
  1.4 3.3 plan.1
  4.7 0.8 reshape.14
  5.5 0.1 copy.12
  5.5 0.1 constant_dynamic-slice_fusion
  5.6 0.1 copy.11
  5.7 0.8 copy.15.occ
  6.5 0.1 copy.14.second_table
  6.6 0.1 copy.13.first_table
  6.7 313.0 %exchange.1 = (bf16[64,2,128,256]{3,2,1,0:T(8,128)(2,1)}, s32[64,1,128]{2,1,0:T(1,128)}, s32[128]{0:T(128)}) custom-call(s32[64]{0:T(128)} %get-tuple-element.9.tile_of_slot, s32[1,1,128]{2,1,0:T(1,128)} %get-tuple-element.10.meta_in, bf16[32,32,1024]{2,1,0:T(8,128)(2,1)} %amplitudes.1, bf16[8,2,1024,256]{3,2,1,0:T(8,128)(2,1)} %integrals.1), custom_call_target="tpu_custom_call" | custom-call | tf_op jit(solution)/shard_map/exchange/pallas_call | solution.py:309
  319.8 0.0 copy-done.1
  319.8 0.0 copy-start
  319.8 3.4 %copy-done = bf16[64,2,128,256]{3,2,1,0:T(8,128)(2,1)S(1)} copy-done((bf16[64,2,128,256]{3,2,1,0:T(8,128)(2,1)S(1)}, bf16[64,2,128,256]{3,2,1,0:T(8,128)(2,1)}, u32[]{:S(2)}) %copy-start) | copy-done | bytes 8388632
  323.1 0.0 copy-start.2
  323.1 0.6 copy-done.2
  323.8 7.4 %combine.1 = bf16[32,128,256]{2,1,0:T(8,128)(2,1)} custom-call(s32[32]{0:T(128)S(1)} %copy-done.1, s32[128]{0:T(128)S(1)} %copy-done.2, bf16[64,2,128,256]{3,2,1,0:T(8,128)(2,1)S(1)} %copy-done, f32[128,256]{1,0:T(8,128)S(1)} %copy.13.first_table, f32[128,256]{1,0:T(8,128)S(1)} %copy.14.second_table, f32[128,1]{1,0:T(8,128)S(1)} %copy.15.occ), custom_call_target="tpu_custom_call" | custom-call | tf_op jit(solution)/shard_map/combine/pallas_call | solution.py:356
  (2 shorter events, 0.0 us)
Async XLA Ops:
  0.0 319.8 %copy-start.1 = (s32[32]{0:T(128)S(1)}, s32[32]{0:T(128)}, u32[]{:S(2)}) copy-start(s32[32]{0:T(128)} %amp_pairs.3) | copy-start | bytes 388
  319.8 3.4 %copy-start = (bf16[64,2,128,256]{3,2,1,0:T(8,128)(2,1)S(1)}, bf16[64,2,128,256]{3,2,1,0:T(8,128)(2,1)}, u32[]{:S(2)}) copy-start(bf16[64,2,128,256]{3,2,1,0:T(8,128)(2,1)} %get-tuple-element.12.returned) | copy-start | bytes 25165828
  323.1 0.6 copy-start.2

commit v3 on v2

--- a/solution.py
+++ b/solution.py
@@ -21,7 +21,7 @@
         meta[0, 0, d] = -1
         return carry
 
-    lax.fori_loop(0, slots, clear, 0)
+    lax.fori_loop(0, slots, clear, 0, unroll=8)
 
     def place(j, carry):
         row = pair_map[amp_pairs[j]]
@@ -34,13 +34,13 @@
 
         return carry
 
-    lax.fori_loop(0, amp_pairs.shape[0], place, 0)
+    lax.fori_loop(0, amp_pairs.shape[0], place, 0, unroll=8)
 
     def copy(i, carry):
         meta[0, 0, slots + i] = block_cols[i]
         return carry
 
-    lax.fori_loop(0, block_cols.shape[0], copy, 0)
+    lax.fori_loop(0, block_cols.shape[0], copy, 0, unroll=8)
 
 
 def exchange_kernel(
@@ -251,7 +251,7 @@
             position[amp_pairs[j]] = j
             return carry
 
-        lax.fori_loop(0, amp_pairs.shape[0], mark, 0)
+        lax.fori_loop(0, amp_pairs.shape[0], mark, 0, unroll=8)
         ladder[...] = jnp.zeros_like(ladder)
 
     def add(i, carry):
@@ -268,13 +268,16 @@
 
     @pl.when(step == pl.num_programs(0) - 1)
     def _():
+        rows = occ.shape[1]
+        occ_column = jnp.transpose(jnp.broadcast_to(occ[...], (rows, rows)))[:, :1]
+
         def divide(j, carry):
             pair = amp_pairs[j]
             energy = (
                 first_table[pl.ds(lax.div(pair, virt_tiles), 1), :]
                 + second_table[pl.ds(lax.rem(pair, virt_tiles), 1), :]
             )
-            update[j] = (ladder[j] / (energy - occ[...])).astype(update.dtype)
+            update[j] = (ladder[j] / (energy - occ_column)).astype(update.dtype)
             return carry
 
         lax.fori_loop(0, amp_pairs.shape[0], divide, 0)
@@ -363,16 +366,16 @@
             pl.BlockSpec((chunk, block_count, occ_rows, part_width), lambda i: (i, 0, 0, 0)),
             whole(virt_tiles, part_width),
             whole(virt_tiles, part_width),
-            whole(occ_rows, 1),
+            whole(1, occ_rows),
         ],
         out_specs=whole(tile_count, occ_rows, part_width),
         scratch_shapes=[
             pltpu.SMEM((pair_map.shape[0],), jnp.int32),
             pltpu.VMEM((tile_count, occ_rows, part_width), jnp.float32),
         ],
-        compiler_params=pltpu.CompilerParams(vmem_limit_bytes=32 * 2**20),
+        compiler_params=pltpu.CompilerParams(vmem_limit_bytes=60 * 2**20),
         name="combine",
-    )(amp_pairs, targets, returned, first_table, second_table, occ_energy[:, None])
+    )(amp_pairs, targets, returned, first_table, second_table, occ_energy[None, :])
 
 
 def solution(mesh):

time: 337 us -> 340 us (level)
  the two profiles are of different devices: /device:TPU:79 before, /device:TPU:127 now
where the time goes in v3:
time: 340 us; the launch traced here: 339 us
  Pallas kernels  335 us (99%)
  local copies, waits for them, and re-layouts  3.91 us (1%)
    pallas_call x1, Pallas kernels, local(): pl.pallas_call(functools.partial(exchange_kernel, pair_dims(n)), out_shap...  322 us
    pallas_call x1, Pallas kernels, local(): pl.pallas_call(functools.partial(combine_kernel, virt_tiles), out_shape=j...  11.2 us

profile of v3, /device:TPU:127, one launch (start us, length us, event | category | flops | bytes accessed | tf_op | source)
XLA Modules:
  0.0 339.3 jit_solution(14048529405349002689)
XLA Ops:
  0.0 0.8 copy.9
  0.8 0.6 reshape.13.block_cols
  1.3 2.6 plan.1
  3.9 0.8 reshape.14
  4.7 0.1 copy.11
  4.8 0.1 constant_dynamic-slice_fusion
  4.9 0.1 copy.10
  5.0 0.8 copy.13.second_table
  5.8 0.8 copy.12.first_table
  6.5 321.5 %exchange.1 = (bf16[64,2,128,256]{3,2,1,0:T(8,128)(2,1)}, s32[64,1,128]{2,1,0:T(1,128)}, s32[128]{0:T(128)}) custom-call(s32[64]{0:T(128)} %get-tuple-element.9.tile_of_slot, s32[1,1,128]{2,1,0:T(1,128)} %get-tuple-element.10.meta_in, bf16[32,32,1024]{2,1,0:T(8,128)(2,1)} %amplitudes.1, bf16[8,2,1024,256]{3,2,1,0:T(8,128)(2,1)} %integrals.1), custom_call_target="tpu_custom_call" | custom-call | tf_op jit(solution)/shard_map/exchange/pallas_call | solution.py:312
  328.0 11.2 %combine.1 = bf16[32,128,256]{2,1,0:T(8,128)(2,1)} custom-call(s32[32]{0:T(128)} %amp_pairs.3, s32[128]{0:T(128)} %get-tuple-element.11.targets, bf16[64,2,128,256]{3,2,1,0:T(8,128)(2,1)} %get-tuple-element.12.returned, f32[128,256]{1,0:T(8,128)} %copy.12.first_table, f32[128,256]{1,0:T(8,128)} %copy.13.second_table, f32[1,128]{1,0:T(1,128)} %bitcast.5), custom_call_target="tpu_custom_call" | custom-call | tf_op jit(solution)/shard_map/combine/pallas_call | solution.py:359
  (2 shorter events, 0.0 us)
